TPU v7x, 128 devices: a whole 4x4x4 slice. The times are simulated.
128 devices in a mesh: row: 8 (over x_hi, y), col: 16 (over x_lo, z, core).
Axes of the slice: x: 4 (x_hi: 2, x_lo: 2; x = x_hi * 2 + x_lo), y: 4, z: 4, core: 2. Of those that a mesh axis runs over, the one named last changes fastest.
Arguments:
- matrix: float32 [32768, 8192], P('row', 'col'), may hold values from -6 to 6
- pivots: int32 [1024], replicated, may hold values from 0 to 32767, as said below
- lower_panel: float32 [1024, 32768], P('col', 'row'), as said below
Outputs:
- updated: float32 [32768, 8192], P('row', 'col')
Inputs may be any that keep to these rules, and one draw needn't show every extreme that they name: `pivots`: the 1024 entries are distinct rows of the trailing matrix. For column index r < 1024: lower_panel[r, r] = 1 and lower_panel[k, r] = 0 for k > r.
All inputs are finite; a program needn't handle non-finite values.
Results may differ from a plain program's by a relative error of at most 0.000059.
Values sent between devices are 32-bit elements; how exact they have to be, the bound alone decides.
No kernel may reach another device: no remote copies, remote signals or barrier semaphores. Data moves between devices by JAX's collectives and lax.ppermute only.
A program may use at most 128 MiB of HBM per device.

v0:
```python
import jax
import jax.numpy as jnp
from jax import lax
from jax.sharding import PartitionSpec as P


def spread(value, axis, source):
    kept = jnp.where(lax.axis_index(axis) == source, value, 0).astype(value.dtype)
    return lax.psum(kept, axis)


def displaced_rows(pivots, top):
    whole = jnp.arange(top, dtype=jnp.int32)
    chosen_top = jnp.any(pivots[None, :] == whole[:, None], axis=1)
    spare_rows = jnp.sort(jnp.where(chosen_top, jnp.int32(2**30), whole))
    vacated = jnp.sort(jnp.where(pivots >= top, pivots, jnp.int32(2**30)))
    return (spare_rows, vacated)


def contract(left_block, right_block):
    return lax.dot_general(
        left_block,
        right_block,
        (((0,), (0,)), ((), ())),
        precision=lax.Precision.HIGHEST,
        preferred_element_type=jnp.float32,
    )


def per_device(matrix, pivots, lower_panel):
    top = pivots.shape[0]
    local_rows, local_cols = matrix.shape
    first_row = lax.axis_index("row") * local_rows
    spare_rows, vacated = displaced_rows(pivots, top)
    initial_top = spread(matrix[:top], "row", 0)
    inside = (vacated >= first_row) & (vacated < first_row + local_rows)
    local_target = jnp.where(inside, vacated - first_row, local_rows)
    swapped = matrix.at[local_target].set(
        initial_top[jnp.minimum(spare_rows, top - 1)], mode="drop"
    )
    owned_mask = (pivots >= first_row) & (pivots < first_row + local_rows)
    local_index = jnp.clip(pivots - first_row, 0, local_rows - 1)
    picked = jnp.where(owned_mask[:, None], jnp.take(matrix, local_index, axis=0), 0.0)
    pivot_block = lax.psum(picked, "row")
    product = contract(lax.all_gather(lower_panel, "col", axis=0, tiled=True), pivot_block)
    global_rows = first_row + jnp.arange(local_rows, dtype=jnp.int32)[:, None]
    return jnp.where(global_rows < top, product, swapped - product)


def solution(mesh):
    in_specs = (P("row", "col"), P(), P("col", "row"))
    out_specs = P("row", "col")
    return jax.shard_map(
        per_device, mesh=mesh, in_specs=in_specs, out_specs=out_specs, check_vma=False
    )
```

profile of v0, /device:TPU:1, one launch (start us, length us, event | category | flops | bytes accessed | tf_op | source)
XLA Modules:
  0.0 292.9 jit_solution(3470179886124595553)
XLA Ops:
  7.4 0.0 all-reduce.3.cloned.1.call-start
  7.4 0.0 copy-start.1
  7.4 7.8 %copy.12 = f32[4096,512]{1,0:T(8,128)} copy(f32[4096,512]{1,0:T(8,128)} %param.3) | data formatting | bytes 16777216
  15.1 0.0 copy-done.1
  15.2 7.4 %gather_fusion = f32[1024,512]{1,0:T(8,128)S(1)} fusion(f32[4096,512]{1,0:T(8,128)} %copy.12, s32[1024]{0:T(1024)S(1)} %get-tuple-element.15), kind=kCustom, calls=%fused_computation | custom fusion | bytes 4198400 | tf_op jit(solution)/shard_map/jit(_take)/gather | solution.py:43
  22.6 3.1 %slice_select_fusion = f32[1024,512]{1,0:T(8,128)} fusion(f32[4096,512]{1,0:T(8,128)} %copy.12, pred[]{:T(512)S(6)} %eq.16), kind=kLoop, calls=%fused_computation.8 | loop fusion | flops 524288 | bytes 4194305 | tf_op jit(solution)/shard_map/jit(_where)/select_n | solution.py:8
  25.7 2.0 select_select_fusion
  27.7 0.0 all-reduce.3.cloned.1.call-update
  27.7 0.0 all-gather.2.cloned.1.call-start
  27.7 0.5 all-gather.2.cloned.1.call-update
  28.3 4.4 %sort.21 = (s32[1024]{0:T(1024)S(1)}, s32[1024]{0:T(1024)}) sort(s32[1024]{0:T(1024)S(1)} %get-tuple-element.16, s32[1024]{0:T(1024)S(1)} %iota.18), dimensions={0}, to_apply=%region_1.2 | sort | flops 10240 | bytes 16384 | tf_op jit(solution)/shard_map/jit(sort)/sort | solution.py:16
  32.6 0.6 fusion
  33.2 4.4 %sort.28 = (s32[1024]{0:T(1024)S(1)}, s32[1024]{0:T(1024)}) sort(s32[1024]{0:T(1024)S(1)} %iota_select_fusion, s32[1024]{0:T(1024)S(1)} %iota.20), dimensions={0}, to_apply=%region_4.5 | sort | flops 10240 | bytes 16384 | tf_op jit(solution)/shard_map/jit(sort)/sort | solution.py:15
  37.6 178.3 %all-reduce.3.cloned.1.call-done = (f32[1024,512]{1,0:T(8,128)}, f32[1024,512]{1,0:T(8,128)}) async-done(((f32[1024,512]{1,0:T(8,128)}, f32[1024,512]{1,0:T(8,128)}), (f32[1024,512]{1,0:T(8,128)}, f32[1024,512]{1,0:T(8,128)})) %all-reduce.3.cloned.1.call-update) | async-done | bytes 4194320 | tf_op jit(solution)/shard_map/psum | solution.py:9
  215.9 20.3 %scatter_custom_fusion = f32[4096,512]{1,0:T(8,128)} fusion(f32[4096,512]{1,0:T(8,128)} %copy.12, s32[1024]{0:T(1024)S(1)} %get-tuple-element.17, f32[1024,512]{1,0:T(8,128)} %get-tuple-element.11, s32[1024]{0:T(1024)S(1)} %get-tuple-element.18), kind=kCustom, calls=%fused_computation.6 | custom fusion | bytes 8388608 | tf_op jit(solution)/shard_map/scatter | solution.py:38
  236.1 0.0 copy-start
  236.1 9.1 %copy.6 = f32[4096,512]{0,1:T(8,128)} copy(f32[4096,512]{1,0:T(8,128)} %scatter_custom_fusion) | data formatting | bytes 16777216 | tf_op jit(solution)/shard_map/scatter | solution.py:38
  245.2 0.0 all-gather.2.cloned.1.call-done
  245.2 0.0 copy-done
  245.2 31.4 %subtract_select_fusion = f32[4096,512]{0,1:T(8,128)} fusion(f32[4096,512]{0,1:T(8,128)} %copy.6, f32[1024,512]{1,0:T(8,128)S(1)} %copy-done, f32[1024,4096]{1,0:T(8,128)} %all-gather.2.cloned.1.call-done, pred[4096]{0:T(1024)(128)(4,1)S(1)} %add_compare_fusion), kind=kOutput, calls=%fused_computation.3 | convolution fusion | flops 25773998080 | bytes 35655680 | tf_op jit(solution)/shard_map/dot_general | solution.py:21
  276.6 8.9 %copy.7 = f32[4096,512]{1,0:T(8,128)} copy(f32[4096,512]{0,1:T(8,128)} %subtract_select_fusion) | data formatting | bytes 16777216 | tf_op jit(solution)/shard_map/jit(_where)/select_n | solution.py:47
  (7 shorter events, 0.1 us)
Async XLA Ops:
  7.4 208.5 %all-reduce.3.cloned.1.call-start = ((), (), s32[]{:S(2)}) async-start(), calls=%async_computation.1 | async-start | bytes 8388608 | tf_op jit(solution)/shard_map/psum | solution.py:9
  7.4 7.8 %copy-start.1 = (s32[1024]{0:T(1024)S(1)}, s32[1024]{0:T(1024)}, u32[]{:S(2)}) copy-start(s32[1024]{0:T(1024)} %param.4) | copy-start | bytes 12292
  27.7 217.5 %all-gather.2.cloned.1.call-start = ((), (), s32[]{:S(2)}) async-start(), calls=%async_computation | async-start | bytes 17825792 | tf_op jit(solution)/shard_map/all_gather | solution.py:45
  236.1 9.1 %copy-start = (f32[1024,512]{1,0:T(8,128)S(1)}, f32[1024,512]{1,0:T(8,128)}, u32[]{:S(2)}) copy-start(f32[1024,512]{1,0:T(8,128)} %get-tuple-element.12) | copy-start | bytes 6291460
Sparse Core Ops, SparseCore 0:
  27.8 187.9 all-reduce.2
Sparse Core Ops, SparseCore 1:
  29.9 131.6 all-gather.1
where the time goes:
time: 294 us; the launch traced here: 293 us
  waiting for transfers between devices  179 us (61%)
  local copies, waits for them, and re-layouts  53.4 us (18%)
  matrix products  31.4 us (11%)
  between operations  14.9 us (5%)
  other arithmetic  14.4 us (5%)
    psum x1, waiting for transfers between devices, spread(): return lax.psum(kept, axis)  178 us
    dot_general x1, matrix products, contract(): lax.dot_general(left_block, right_block, (((0,), (0,)), ((), ())), precis...  31.4 us
    scatter x2, local copies, waits for them, and re-layouts, per_device(): matrix.at[local_target]  29.3 us
    select_n x1, local copies, waits for them, and re-layouts, per_device(): return jnp.where(global_rows < top, product, swapped - product)  8.94 us
    unnamed x5, local copies, waits for them, and re-layouts  7.78 us
    gather x1, local copies, waits for them, and re-layouts, per_device(): jnp.take(matrix, local_index, axis=0)  7.4 us
  transfers between devices with their start and end apart: 2, of which 1 were waited for; matrix products, arithmetic and copies ran while one was open for 13% of the time, Pallas kernels for 0%

commit v1 on v0

--- a/solution.py
+++ b/solution.py
@@ -2,11 +2,16 @@
 import jax.numpy as jnp
 from jax import lax
 from jax.sharding import PartitionSpec as P
+from jax.lax import all_gather
 
 
 def spread(value, axis, source):
     kept = jnp.where(lax.axis_index(axis) == source, value, 0).astype(value.dtype)
-    return lax.psum(kept, axis)
+
+    def build_bands_here(sheet):
+        return all_gather(sheet, axis_name=axis).sum(axis=0)
+
+    return build_bands_here(kept)
 
 
 def displaced_rows(pivots, top):

time: 294 us -> 437 us (1.49)
  waiting for transfers between devices: 179 us -> 319 us
  other arithmetic: 14.4 us -> 22.5 us
  local copies, waits for them, and re-layouts: 53.4 us -> 48.9 us
    all_gather x0 -> x1, waiting for transfers between devices: none -> 165 us  [build_bands_here(): return all_gather(sheet, axis_name=axis).sum(axis=0)]
    psum x1, waiting for transfers between devices: 178 us -> 56.9 us  [per_device(): pivot_block = lax.psum(picked, 'row')]
    all_gather x1, waiting for transfers between devices: 0.01 us -> 97.2 us  [per_device(): lax.all_gather(lower_panel, 'col', axis=0, tiled=True)]
    reduce_sum x0 -> x1, other arithmetic: none -> 8.08 us  [build_bands_here(): return all_gather(sheet, axis_name=axis).sum(axis=0)]
    scatter x2, local copies, waits for them, and re-layouts: 29.3 us -> 24.2 us  [per_device(): matrix.at[local_target]]
  transfers between devices with their start and end apart: 2 -> 3, of which waited for: 1 -> 3; matrix products, arithmetic and copies ran while one was open for 13% -> 12% of each run, Pallas kernels for 0% -> 0%
where the time goes in v1:
time: 437 us; the launch traced here: 436 us
  waiting for transfers between devices  319 us (73%)
  local copies, waits for them, and re-layouts  48.9 us (11%)
  matrix products  31.9 us (7%)
  other arithmetic  22.5 us (5%)
  between operations  13.2 us (3%)
    all_gather x1, waiting for transfers between devices, build_bands_here(): return all_gather(sheet, axis_name=axis).sum(axis=0)  165 us
    all_gather x1, waiting for transfers between devices, per_device(): lax.all_gather(lower_panel, 'col', axis=0, tiled=True)  97.2 us
    psum x1, waiting for transfers between devices, per_device(): pivot_block = lax.psum(picked, 'row')  56.9 us
    dot_general x1, matrix products, contract(): lax.dot_general(left_block, right_block, (((0,), (0,)), ((), ())), precis...  31.9 us
    scatter x2, local copies, waits for them, and re-layouts, per_device(): matrix.at[local_target]  24.2 us
    select_n x1, local copies, waits for them, and re-layouts, per_device(): return jnp.where(global_rows < top, product, swapped - product)  8.94 us
  transfers between devices with their start and end apart: 3, of which 3 were waited for; matrix products, arithmetic and copies ran while one was open for 12% of the time, Pallas kernels for 0%

profile of v1, /device:TPU:1, one launch (start us, length us, event | category | flops | bytes accessed | tf_op | source)
XLA Modules:
  0.0 436.1 jit_solution(6153441311114188784)
XLA Ops:
  6.5 0.0 all-gather.6.cloned.1.call-start
  6.5 7.8 %copy.11 = f32[4096,512]{1,0:T(8,128)} copy(f32[4096,512]{1,0:T(8,128)} %param.3) | data formatting | bytes 16777216
  14.3 3.1 slice_select_fusion
  17.4 0.0 copy-start
  17.4 0.0 all-gather.6.cloned.1.call-update
  17.4 0.0 all-reduce.2.cloned.1.call-start
  17.5 0.6 copy-done
  18.1 7.4 %gather_fusion = f32[1024,512]{1,0:T(8,128)S(1)} fusion(f32[4096,512]{1,0:T(8,128)} %copy.11, s32[1024]{0:T(1024)S(1)} %get-tuple-element.13), kind=kCustom, calls=%fused_computation | custom fusion | bytes 4198400 | tf_op jit(solution)/shard_map/jit(_take)/gather | solution.py:48
  25.5 2.0 select_select_fusion
  27.5 0.0 all-reduce.2.cloned.1.call-update
  27.5 0.0 all-gather.4.cloned.1.call-start
  27.6 0.7 all-gather.4.cloned.1.call-update
  28.3 4.4 %sort.21 = (s32[1024]{0:T(1024)S(1)}, s32[1024]{0:T(1024)}) sort(s32[1024]{0:T(1024)S(1)} %get-tuple-element.14, s32[1024]{0:T(1024)S(1)} %iota.18), dimensions={0}, to_apply=%region_1.2 | sort | flops 10240 | bytes 16384 | tf_op jit(solution)/shard_map/jit(sort)/sort | solution.py:21
  32.7 0.6 fusion
  33.2 4.4 %sort.28 = (s32[1024]{0:T(1024)S(1)}, s32[1024]{0:T(1024)}) sort(s32[1024]{0:T(1024)S(1)} %iota_select_fusion, s32[1024]{0:T(1024)S(1)} %iota.20), dimensions={0}, to_apply=%region_4.5 | sort | flops 10240 | bytes 16384 | tf_op jit(solution)/shard_map/jit(sort)/sort | solution.py:20
  37.6 164.5 %all-gather.6.cloned.1.call-done = f32[8192,512]{1,0:T(8,128)} async-done(((f32[1024,512]{1,0:T(8,128)}), f32[8192,512]{1,0:T(8,128)}) %all-gather.6.cloned.1.call-update) | async-done | bytes 16777232 | tf_op jit(solution)/shard_map/all_gather | solution.py:12
  202.2 8.1 %reduce_sum.9 = f32[1024,512]{1,0:T(8,128)S(1)} reduce(f32[8,1024,512]{2,1,0:T(8,128)} %bitcast.5, f32[]{:T(128)} %constant.18.clone.1), dimensions={0}, to_apply=%region_2.3 | reduce | flops 3670016 | bytes 18874372 | tf_op jit(solution)/shard_map/reduce_sum | solution.py:12
  210.2 15.3 %scatter_custom_fusion = f32[4096,512]{1,0:T(8,128)} fusion(f32[4096,512]{1,0:T(8,128)} %copy.11, s32[1024]{0:T(1024)S(1)} %compare_select_fusion.1, f32[1024,512]{1,0:T(8,128)S(1)} %reduce_sum.9, s32[1024]{0:T(1024)S(1)} %fusion.3), kind=kCustom, calls=%fused_computation.6 | custom fusion | bytes 8388608 | tf_op jit(solution)/shard_map/scatter | solution.py:43
  225.5 8.9 %copy.6 = f32[4096,512]{0,1:T(8,128)} copy(f32[4096,512]{1,0:T(8,128)} %scatter_custom_fusion) | data formatting | bytes 16777216 | tf_op jit(solution)/shard_map/scatter | solution.py:43
  234.5 56.9 %all-reduce.2.cloned.1.call-done = f32[1024,512]{1,0:T(8,128)} async-done(((f32[1024,512]{1,0:T(8,128)}), f32[1024,512]{1,0:T(8,128)}) %all-reduce.2.cloned.1.call-update) | async-done | bytes 2097168 | tf_op jit(solution)/shard_map/psum | solution.py:49
  291.4 97.2 %all-gather.4.cloned.1.call-done = f32[1024,4096]{1,0:T(8,128)} async-done(((f32[64,4096]{1,0:T(8,128)}), f32[1024,4096]{1,0:T(8,128)}) %all-gather.4.cloned.1.call-update) | async-done | bytes 16777232 | tf_op jit(solution)/shard_map/all_gather | solution.py:50
  388.7 31.9 %subtract_select_fusion = f32[4096,512]{0,1:T(8,128)} fusion(f32[4096,512]{0,1:T(8,128)} %copy.6, f32[1024,512]{1,0:T(8,128)} %all-reduce.2.cloned.1.call-done, f32[1024,4096]{1,0:T(8,128)} %all-gather.4.cloned.1.call-done, pred[4096]{0:T(1024)(128)(4,1)S(1)} %add_compare_fusion), kind=kOutput, calls=%fused_computation.3 | convolution fusion | flops 25773998080 | bytes 35655680 | tf_op jit(solution)/shard_map/dot_general | solution.py:26
  420.6 8.9 %copy.7 = f32[4096,512]{1,0:T(8,128)} copy(f32[4096,512]{0,1:T(8,128)} %subtract_select_fusion) | data formatting | bytes 16777216 | tf_op jit(solution)/shard_map/jit(_where)/select_n | solution.py:52
  (8 shorter events, 0.1 us)
Async XLA Ops:
  6.5 195.6 %all-gather.6.cloned.1.call-start = ((), (), s32[]{:S(2)}) async-start(), calls=%async_computation.2 | async-start | bytes 18874368 | tf_op jit(solution)/shard_map/all_gather | solution.py:12
  17.4 0.7 copy-start
  17.4 274.0 %all-reduce.2.cloned.1.call-start = ((), (), s32[]{:S(2)}) async-start(), calls=%async_computation | async-start | bytes 4194304 | tf_op jit(solution)/shard_map/psum | solution.py:49
  27.5 361.1 %all-gather.4.cloned.1.call-start = ((), (), s32[]{:S(2)}) async-start(), calls=%async_computation.1 | async-start | bytes 17825792 | tf_op jit(solution)/shard_map/all_gather | solution.py:50
Sparse Core Ops, SparseCore 0:
  17.6 184.5 all-gather.5
  204.7 86.7 all-reduce.1
  293.1 95.4 all-gather.3
